TPU v7x, 32 devices: a whole 2x2x4 slice. The times are simulated.
32 devices in a mesh: seq: 4 (over y, x), fsdp: 8 (over z, core).
Axes of the slice: x: 2, y: 2, z: 4, core: 2. Of those that a mesh axis runs over, the one named last changes fastest.
Arguments:
- block_input: bfloat16 [8, 2048, 1024], P('fsdp', 'seq'), may hold values from -6 to 6
- norm_gain_a: float32 [1024], P('fsdp'), may hold values from 0.1 to 1.9
- weight_qkv: float32 [1024, 3072], P('fsdp'), may hold values from -0.1875 to 0.1875
- weight_out: float32 [1024, 1024], P('fsdp'), may hold values from -3 to 3
- norm_gain_b: float32 [1024], P('fsdp'), may hold values from 0.1 to 1.9
- weight_gate_up: float32 [1024, 8192], P('fsdp'), may hold values from -0.1875 to 0.1875
- weight_down: float32 [1024, 4096], P('fsdp'), may hold values from -0.09375 to 0.09375
- cotangent: bfloat16 [8, 2048, 1024], P('fsdp', 'seq'), may hold values from -6 to 6
- permutation: int32 [8, 2048], P('fsdp'), may hold values from 0 to 2047, each once within a row
- lengths: int32 [8, 3], P('fsdp'), may hold values from 256 to 1024, as said below
- offsets: int32 [8, 3], P('fsdp'), may hold values from 0 to 1792, as said below
Outputs:
- block_output: bfloat16 [8, 2048, 1024], P('fsdp', 'seq')
- grad_input: bfloat16 [8, 2048, 1024], P('fsdp', 'seq')
- grad_gain_a: float32 [1024], P('fsdp')
- grad_qkv: float32 [1024, 3072], P('fsdp')
- grad_out: float32 [1024, 1024], P('fsdp')
- grad_gain_b: float32 [1024], P('fsdp')
- grad_gate_up: float32 [1024, 8192], P('fsdp')
- grad_down: float32 [1024, 4096], P('fsdp')
Inputs may be any that keep to these rules, and one draw needn't show every extreme that they name: A group's 3 lengths sum to 2048, and its longest is exactly 1024. offsets[g, k] is the sum of lengths[g, i] over i < k, so that a group's sequences tile its positions.
All inputs are finite; a program needn't handle non-finite values.
Results may differ from a plain program's by a relative error of at most 0.02.
Values may be sent and summed in bfloat16 or wider, within the bound.
A program may use at most 256 MiB of HBM per device.

v0:
```python
import jax
import jax.numpy as jnp
from jax import lax
from jax.sharding import PartitionSpec as P

HEADS = 16
HEAD_DIM = 64
epsilon = 1e-05


def rms_scale(values):
    return lax.rsqrt(jnp.mean(values * values, axis=-1, keepdims=True) + epsilon)


def norm_backward(values, inv_scale, grad_normed, gain):
    scaled = grad_normed * gain
    gain_grad = jnp.sum(grad_normed * values * inv_scale, axis=0)
    input_grad = inv_scale * scaled - values * inv_scale**3 * jnp.mean(
        values * scaled, axis=-1, keepdims=True
    )
    return (input_grad, gain_grad)


def block_mask(seg_query, pos_query, segment, position):
    return (seg_query[:, None] == segment[None, :]) & (position[None, :] <= pos_query[:, None])


def on_device(
    block_input,
    norm_gain_a,
    weight_qkv,
    weight_out,
    norm_gain_b,
    weight_gate_up,
    weight_down,
    cotangent,
    permutation,
    lengths,
    offsets,
):
    seq_count = lax.axis_size("seq")
    row_count = block_input.shape[1]
    model_width = block_input.shape[2]
    group_len = row_count * seq_count
    head_local = HEADS // seq_count
    score_scale = HEAD_DIM ** (-0.5)
    blk_rows = min(512, group_len)
    block_count = group_len // blk_rows
    inputs = block_input[0].astype(jnp.float32)
    gain_a, full_qkv, full_out = (
        lax.all_gather(norm_gain_a.astype(jnp.bfloat16), "fsdp", axis=0, tiled=True),
        lax.all_gather(weight_qkv.astype(jnp.bfloat16), "fsdp", axis=0, tiled=True),
        lax.all_gather(weight_out.astype(jnp.bfloat16), "fsdp", axis=0, tiled=True),
    )
    inv_first = rms_scale(inputs)
    normed_a = (inputs * inv_first * gain_a.astype(jnp.float32)).astype(jnp.bfloat16)
    qkv_rows = jnp.dot(normed_a, full_qkv, preferred_element_type=jnp.float32).astype(jnp.bfloat16)
    head_rows = lax.all_to_all(
        qkv_rows.reshape(row_count, 3, seq_count, -1),
        "seq",
        split_axis=2,
        concat_axis=0,
        tiled=True,
    )
    head_rows = head_rows.reshape(group_len, 3, head_local, HEAD_DIM)
    position = jnp.arange(group_len, dtype=jnp.int32)
    dealt_pos = permutation[0]
    inverse = jnp.zeros((group_len,), jnp.int32).at[dealt_pos].set(position)
    ordered = head_rows[inverse]
    seq_starts = offsets[0]
    seq_lengths = lengths[0]
    inside = (position[:, None] >= seq_starts[None, :]) & (
        position[:, None] < seq_starts[None, :] + seq_lengths[None, :]
    )
    segment = jnp.sum(
        inside.astype(jnp.int32) * jnp.arange(seq_lengths.shape[0], dtype=jnp.int32)[None, :],
        axis=1,
    )
    queries = ordered[:, 0]
    key_rows = ordered[:, 1]
    values = ordered[:, 2]

    def forward_block(block_item):
        query_blk, seg_blk, pos_blk = block_item
        scores = (
            jnp.einsum("qhd,khd->hqk", query_blk, key_rows, preferred_element_type=jnp.float32)
            * score_scale
        )
        allowed = block_mask(seg_blk, pos_blk, segment, position)
        scores = jnp.where(allowed[None], scores, -1e30)
        row_top = jnp.max(scores, axis=-1, keepdims=True)
        exponent = jnp.exp(scores - row_top)
        row_total = jnp.sum(exponent, axis=-1, keepdims=True)
        weights_low = (exponent / row_total).astype(jnp.bfloat16)
        attended = jnp.einsum(
            "hqk,khd->qhd", weights_low, values, preferred_element_type=jnp.float32
        )
        return (attended.astype(jnp.bfloat16), (row_top + jnp.log(row_total))[:, :, 0])

    query_blocks = queries.reshape(block_count, blk_rows, head_local, HEAD_DIM)
    seg_blocks = segment.reshape(block_count, blk_rows)
    pos_blocks = position.reshape(block_count, blk_rows)
    attended, log_total = lax.map(forward_block, (query_blocks, seg_blocks, pos_blocks))
    dealt_out = attended.reshape(group_len, -1)[dealt_pos]
    mixed = lax.all_to_all(
        dealt_out.reshape(group_len, 1, -1), "seq", split_axis=0, concat_axis=1, tiled=True
    ).reshape(row_count, model_width)
    hidden = inputs + jnp.dot(mixed, full_out, preferred_element_type=jnp.float32)
    gain_b, full_gate_up, full_down = (
        lax.all_gather(norm_gain_b.astype(jnp.bfloat16), "fsdp", axis=0, tiled=True),
        lax.all_gather(weight_gate_up.astype(jnp.bfloat16), "fsdp", axis=0, tiled=True),
        lax.all_gather(weight_down.astype(jnp.bfloat16), "fsdp", axis=0, tiled=True),
    )
    inv_second = rms_scale(hidden)
    normed_b = (hidden * inv_second * gain_b.astype(jnp.float32)).astype(jnp.bfloat16)
    gate_up = jnp.dot(normed_b, full_gate_up, preferred_element_type=jnp.float32)
    hidden_units = full_gate_up.shape[1] // 2
    gate_part = gate_up[:, :hidden_units]
    up_part = gate_up[:, hidden_units:]
    gate_sigmoid = jax.nn.sigmoid(gate_part)
    gate_silu = gate_part * gate_sigmoid
    activation = (gate_silu * up_part).astype(jnp.bfloat16)
    branch_out = jnp.einsum("rf,df->rd", activation, full_down, preferred_element_type=jnp.float32)
    result_rows = (hidden + branch_out).astype(jnp.bfloat16)
    gain_b, full_gate_up, full_down = (
        lax.all_gather(norm_gain_b.astype(jnp.bfloat16), "fsdp", axis=0, tiled=True),
        lax.all_gather(weight_gate_up.astype(jnp.bfloat16), "fsdp", axis=0, tiled=True),
        lax.all_gather(weight_down.astype(jnp.bfloat16), "fsdp", axis=0, tiled=True),
    )
    out_grad = cotangent[0].astype(jnp.float32)
    out_grad_low = out_grad.astype(jnp.bfloat16)
    grad_down_term = jnp.einsum(
        "rd,rf->df", out_grad_low, activation, preferred_element_type=jnp.float32
    )
    grad_activation = jnp.dot(out_grad_low, full_down, preferred_element_type=jnp.float32)
    grad_gate = grad_activation * up_part * gate_sigmoid * (1.0 + gate_part * (1.0 - gate_sigmoid))
    grad_up = grad_activation * gate_silu
    grad_gate_up = jnp.concatenate([grad_gate, grad_up], axis=1).astype(jnp.bfloat16)
    grad_gate_up_term = jnp.einsum(
        "rd,rf->df", normed_b, grad_gate_up, preferred_element_type=jnp.float32
    )
    grad_normed_b = jnp.einsum(
        "rf,df->rd", grad_gate_up, full_gate_up, preferred_element_type=jnp.float32
    )
    hidden_back, grad_gain_b_term = norm_backward(
        hidden, inv_second, grad_normed_b, gain_b.astype(jnp.float32)
    )
    grad_hidden = out_grad + hidden_back
    gain_a, full_qkv, full_out = (
        lax.all_gather(norm_gain_a.astype(jnp.bfloat16), "fsdp", axis=0, tiled=True),
        lax.all_gather(weight_qkv.astype(jnp.bfloat16), "fsdp", axis=0, tiled=True),
        lax.all_gather(weight_out.astype(jnp.bfloat16), "fsdp", axis=0, tiled=True),
    )
    grad_branch = grad_hidden.astype(jnp.bfloat16)
    grad_out_term = jnp.einsum("rd,re->de", mixed, grad_branch, preferred_element_type=jnp.float32)
    grad_mixed = jnp.einsum(
        "re,de->rd", grad_branch, full_out, preferred_element_type=jnp.float32
    ).astype(jnp.bfloat16)
    grad_heads = lax.all_to_all(
        grad_mixed.reshape(row_count, seq_count, -1), "seq", split_axis=1, concat_axis=0, tiled=True
    )
    grad_ordered = grad_heads.reshape(group_len, head_local, HEAD_DIM)[inverse]
    grad_blocks = grad_ordered.reshape(block_count, blk_rows, head_local, HEAD_DIM)

    def backward_block(carry, block_item):
        key_acc, value_acc = carry
        query_blk, grad_blk, log_blk, seg_blk, pos_blk = block_item
        scores = (
            jnp.einsum("qhd,khd->hqk", query_blk, key_rows, preferred_element_type=jnp.float32)
            * score_scale
        )
        allowed = block_mask(seg_blk, pos_blk, segment, position)
        scores = jnp.where(allowed[None], scores, -1e30)
        probability = jnp.exp(scores - log_blk[:, :, None])
        grad_prob = jnp.einsum("qhd,khd->hqk", grad_blk, values, preferred_element_type=jnp.float32)
        row_delta = jnp.sum(probability * grad_prob, axis=-1, keepdims=True)
        grad_score = (probability * (grad_prob - row_delta)).astype(jnp.bfloat16)
        grad_query = (
            jnp.einsum("hqk,khd->qhd", grad_score, key_rows, preferred_element_type=jnp.float32)
            * score_scale
        )
        key_acc = (
            key_acc
            + jnp.einsum("hqk,qhd->khd", grad_score, query_blk, preferred_element_type=jnp.float32)
            * score_scale
        )
        value_acc = value_acc + jnp.einsum(
            "hqk,qhd->khd",
            probability.astype(jnp.bfloat16),
            grad_blk,
            preferred_element_type=jnp.float32,
        )
        return ((key_acc, value_acc), grad_query.astype(jnp.bfloat16))

    zero_acc = jnp.zeros((group_len, head_local, HEAD_DIM), jnp.float32)
    accumulated, query_grad = lax.scan(
        backward_block,
        (zero_acc, zero_acc),
        (query_blocks, grad_blocks, log_total, seg_blocks, pos_blocks),
    )
    qkv_grad = jnp.stack(
        [
            query_grad.reshape(group_len, -1),
            accumulated[0].reshape(group_len, -1).astype(jnp.bfloat16),
            accumulated[1].reshape(group_len, -1).astype(jnp.bfloat16),
        ],
        axis=1,
    )
    dealt_grad = qkv_grad[dealt_pos]
    rows_grad = lax.all_to_all(
        dealt_grad.reshape(group_len, 3, 1, -1), "seq", split_axis=0, concat_axis=2, tiled=True
    ).reshape(row_count, -1)
    grad_qkv_term = jnp.einsum("rd,re->de", normed_a, rows_grad, preferred_element_type=jnp.float32)
    grad_normed_a = jnp.einsum("re,de->rd", rows_grad, full_qkv, preferred_element_type=jnp.float32)
    input_back, grad_gain_a_term = norm_backward(
        inputs, inv_first, grad_normed_a, gain_a.astype(jnp.float32)
    )
    input_grad = (grad_hidden + input_back).astype(jnp.bfloat16)
    attn_shards = (
        lax.psum_scatter(
            grad_gain_a_term.astype(jnp.bfloat16), "fsdp", scatter_dimension=0, tiled=True
        ).astype(jnp.float32),
        lax.psum_scatter(
            grad_qkv_term.astype(jnp.bfloat16), "fsdp", scatter_dimension=0, tiled=True
        ).astype(jnp.float32),
        lax.psum_scatter(
            grad_out_term.astype(jnp.bfloat16), "fsdp", scatter_dimension=0, tiled=True
        ).astype(jnp.float32),
    )
    mlp_shards = (
        lax.psum_scatter(
            grad_gain_b_term.astype(jnp.bfloat16), "fsdp", scatter_dimension=0, tiled=True
        ).astype(jnp.float32),
        lax.psum_scatter(
            grad_gate_up_term.astype(jnp.bfloat16), "fsdp", scatter_dimension=0, tiled=True
        ).astype(jnp.float32),
        lax.psum_scatter(
            grad_down_term.astype(jnp.bfloat16), "fsdp", scatter_dimension=0, tiled=True
        ).astype(jnp.float32),
    )
    totals = (
        lax.psum(attn_shards[0].astype(jnp.bfloat16), "seq").astype(jnp.float32),
        lax.psum(attn_shards[1].astype(jnp.bfloat16), "seq").astype(jnp.float32),
        lax.psum(attn_shards[2].astype(jnp.bfloat16), "seq").astype(jnp.float32),
        lax.psum(mlp_shards[0].astype(jnp.bfloat16), "seq").astype(jnp.float32),
        lax.psum(mlp_shards[1].astype(jnp.bfloat16), "seq").astype(jnp.float32),
        lax.psum(mlp_shards[2].astype(jnp.bfloat16), "seq").astype(jnp.float32),
    )
    return (
        result_rows[None],
        input_grad[None],
        totals[0],
        totals[1],
        totals[2],
        totals[3],
        totals[4],
        totals[5],
    )


def solution(mesh):
    placed = (
        P("fsdp", "seq", None),
        P("fsdp"),
        P("fsdp", None),
        P("fsdp", None),
        P("fsdp"),
        P("fsdp", None),
        P("fsdp", None),
        P("fsdp", "seq", None),
        P("fsdp", None),
        P("fsdp", None),
        P("fsdp", None),
    )
    return jax.shard_map(
        on_device,
        mesh=mesh,
        in_specs=placed,
        out_specs=(
            P("fsdp", "seq", None),
            P("fsdp", "seq", None),
            P("fsdp"),
            P("fsdp", None),
            P("fsdp", None),
            P("fsdp"),
            P("fsdp", None),
            P("fsdp", None),
        ),
        check_vma=False,
    )
```

profile of v0, /device:TPU:0, one launch (start us, length us, event | category | flops | bytes accessed | tf_op | source)
XLA Modules:
  0.0 1127.1 jit_solution(276207675843231154)
XLA Ops:
  15.4 13.5 %all-gather = bf16[8,1,128]{2,1,0:T(2,128)(2,1)S(1)} all-gather(bf16[1,1,128]{2,1,0:T(2,128)(2,1)S(1)} %convert_bitcast_fusion.3), channel_id=1, replica_groups=mesh['seq'=4,'fsdp'=8] {'fsdp'}, dimensions={0}, use_global_device_ids=true | all-gather | bytes 2304 | tf_op jit(solution)/shard_map/all_gather | solution.py:51
  29.8 47.9 %all-gather.7.cloned.1.call-done = bf16[1024,3072]{1,0:T(8,128)(2,1)} async-done(((bf16[128,3072]{1,0:T(8,128)(2,1)}), bf16[1024,3072]{1,0:T(8,128)(2,1)}) %all-gather.7.cloned.1.call-update) | async-done | bytes 6291472 | tf_op jit(solution)/shard_map/all_gather | solution.py:52
  77.7 7.7 convolution_convert_fusion.2
  102.6 8.5 scatter_custom_fusion
  112.3 23.5 %all-to-all-done = bf16[512,3,4,256]{0,3,1,2:T(8,128)(2,1)S(1)} async-done(((bf16[512,3,4,256]{0,3,1,2:T(8,128)(2,1)}), bf16[512,3,4,256]{0,3,1,2:T(8,128)(2,1)S(1)}, u32[]{:S(2)}, u32[]{:S(2)}) %all-to-all-start) | async-done | bytes 3145760 | tf_op jit(solution)/shard_map/all_to_all | solution.py:58
  140.4 13.1 %reshape.380 = bf16[2048,3,4,64]{3,2,1,0:T(4,128)(2,1)} reshape(bf16[4,512,3,1,256]{4,2,1,0,3:T(4,128)(2,1)} %copy.141) | data formatting | bytes 6291456 | tf_op jit(solution)/shard_map/reshape | solution.py:65
  153.6 23.0 %gather_fusion = bf16[2048,3,4,64]{3,2,1,0:T(4,128)(2,1)} fusion(bf16[2048,3,4,64]{3,2,1,0:T(4,128)(2,1)} %reshape.380, s32[2048]{0:T(1024)S(1)} %fusion.84), kind=kCustom, calls=%fused_computation | custom fusion | bytes 6299648 | tf_op jit(solution)/shard_map/gather | solution.py:69
  191.8 64.2 %while.28 = (s32[]{:T(128)}, bf16[4,512,4,64]{1,3,2,0:T(8,128)(2,1)}, f32[4,4,512]{2,1,0:T(4,128)}, s32[4,512]{1,0:T(4,128)}, s32[2048]{0:T(1024)S(1)}, /*index=...) while((s32[]{:T(128)}, ...), condition=%wide.region_6.7_spmd.clone, body=%wide.region_3.6_spmd.clone.sunk | while | flops 1127348224 | bytes 57233532 | solution.py:103
  264.6 9.1 gather_fusion.1
  282.9 9.8 all-gather.1
  310.1 18.8 %fusion.89 = f32[512,8192]{1,0:T(8,128)} fusion(bf16[1024,8192]{1,0:T(8,128)(2,1)} %all-gather.11.cloned.1.call-done, f32[512,1024]{1,0:T(8,128)} %get-tuple-element.422, f32[1024]{0:T(1024)S(1)} %bitcast.234, f32[512]{0:T(512)S(1)} %get-tuple-element.420), kind=kOutput, calls=%fused_computation.139 | convolution fusion | flops 8591507456 | bytes 35657728 | tf_op jit(solution)/shard_map/dot_general | solution.py:116
  328.9 13.4 %all-gather.13.cloned.1.call-done = bf16[1024,4096]{1,0:T(8,128)(2,1)} async-done(((bf16[128,4096]{1,0:T(8,128)(2,1)}), bf16[1024,4096]{1,0:T(8,128)(2,1)}) %all-gather.13.cloned.1.call-update) | async-done | bytes 8388624 | tf_op jit(solution)/shard_map/all_gather | solution.py:112
  342.3 15.1 %multiply_convert_fusion.2 = (bf16[512,4096]{1,0:T(8,128)(2,1)}, bf16[512,4096]{1,0:T(8,128)(2,1)}, bf16[512,4096]{1,0:T(8,128)(2,1)S(1)}) fusion(f32[512,8192]{1,0:T(8,128)} %fusion.89, bf16[1024,4096]{1,0:T(8,128)(2,1)} %all-gather.13.cloned.1.call-done, bf16[1,512,1024]{2,1,0:T(8,128)(2,1)S(1)} %copy-done.22), kind=kOutput, calls=%fused_computation.67 | convolution fusion | flops 4326424576 | bytes 38797312 | tf_op jit(solution)/shard_map/dot_general | solution.py:135
  359.4 6.8 convert_bitcast_fusion
  366.2 11.7 %copy.151 = bf16[1024,4096]{1,0:T(8,128)(2,1)} copy(bf16[1024,4096]{0,1:T(8,128)(2,1)} %convert_bitcast_fusion) | data formatting | bytes 16777216
  377.9 18.0 %multiply_reduce_fusion.1 = (bf16[1024]{0:T(1024)(128)(2,1)}, f32[512]{0:T(512)S(1)}, f32[512,1024]{1,0:T(8,128)}) fusion(f32[512,1024]{1,0:T(8,128)} %get-tuple-element.422, f32[512]{0:T(512)S(1)} %get-tuple-element.420, f32[1024]{0:T(1024)S(1)} %bitcast.235, bf16[1024,8192]{1,0:T(8,128)(2,1)} %all-gather.11.cloned.1.call-done, ...), kind=kOutput, calls=%fused_computation.97 | convolution fusion | flops 8609855488 | bytes 29370368 | tf_op jit(solution)/shard_map/rf,df->rd/dot_general | solution.py:142
  411.2 9.6 all-to-all-done.2
  425.0 16.1 %gather_fusion.2 = bf16[2048,4,64]{2,1,0:T(4,128)(2,1)} fusion(bf16[2048,4,64]{2,1,0:T(4,128)(2,1)} %reshape.382, s32[2048]{0:T(1024)S(1)} %copy-done.27), kind=kCustom, calls=%fused_computation.2 | custom fusion | bytes 2105344 | tf_op jit(solution)/shard_map/gather | solution.py:162
  446.2 209.1 %while.29 = (s32[]{:T(128)}, f32[2048,4,64]{0,2,1:T(8,128)}, f32[2048,4,64]{0,2,1:T(8,128)}, bf16[4,512,4,64]{1,3,2,0:T(8,128)(2,1)}, bf16[4,512,4,64]{1,3,2,0:T...) while((s32[]{:T(128)}, f32[2048,4,64]{0,2,1:T(8,128)}, ...), condition=%wide.region_11.12_spmd.clone, body=%wide.region_9.11_spmd.clone.sunk | while | flops 2753296384 | bytes 268841472 | solution.py:196
  454.4 12.3 %multiply_reduce_fusion.5 = (f32[4,512]{1,0:T(4,128)}, f32[4,512,2048]{2,1,0:T(8,128)}) fusion(f32[4,512,2048]{2,1,0:T(8,128)S(1)} %fusion.146, f32[4,512]{1,0:T(4,128)S(1)} %dynamic-slice_bitcast_fusion.2, pred[512,2048]{1,0:T(8,128)(4,1)S(1)} %fusion.147, bf16[2048,4,64]{0,2,1:T(8,128)(2,1)} %get-tuple-element.638, ...), kind=kOutput, calls=%fused_computation.28.clone.1 | convolution fusion | flops 557840384 | bytes 35930116 | tf_op jit(solution)/shard_map/while/body/eval_jaxpr/qhd,khd->hqk/dot_general | solution.py:175
  466.7 11.0 multiply_convert_fusion.8
  477.7 6.7 fusion.148
  484.4 8.6 fusion.149
  506.3 12.3 %multiply_reduce_fusion.5 = (f32[4,512]{1,0:T(4,128)}, f32[4,512,2048]{2,1,0:T(8,128)}) fusion(f32[4,512,2048]{2,1,0:T(8,128)S(1)} %fusion.146, f32[4,512]{1,0:T(4,128)S(1)} %dynamic-slice_bitcast_fusion.2, pred[512,2048]{1,0:T(8,128)(4,1)S(1)} %fusion.147, bf16[2048,4,64]{0,2,1:T(8,128)(2,1)} %get-tuple-element.638, ...), kind=kOutput, calls=%fused_computation.28.clone.1 | convolution fusion | flops 557840384 | bytes 35930116 | tf_op jit(solution)/shard_map/while/body/eval_jaxpr/qhd,khd->hqk/dot_general | solution.py:175
  518.6 10.9 multiply_convert_fusion.8
  529.6 7.2 fusion.148
  536.8 8.5 fusion.149
  558.5 12.3 %multiply_reduce_fusion.5 = (f32[4,512]{1,0:T(4,128)}, f32[4,512,2048]{2,1,0:T(8,128)}) fusion(f32[4,512,2048]{2,1,0:T(8,128)S(1)} %fusion.146, f32[4,512]{1,0:T(4,128)S(1)} %dynamic-slice_bitcast_fusion.2, pred[512,2048]{1,0:T(8,128)(4,1)S(1)} %fusion.147, bf16[2048,4,64]{0,2,1:T(8,128)(2,1)} %get-tuple-element.638, ...), kind=kOutput, calls=%fused_computation.28.clone.1 | convolution fusion | flops 557840384 | bytes 35930116 | tf_op jit(solution)/shard_map/while/body/eval_jaxpr/qhd,khd->hqk/dot_general | solution.py:175
  570.8 10.9 multiply_convert_fusion.8
  581.8 7.2 fusion.148
  589.0 8.5 fusion.149
  610.7 12.3 %multiply_reduce_fusion.5 = (f32[4,512]{1,0:T(4,128)}, f32[4,512,2048]{2,1,0:T(8,128)}) fusion(f32[4,512,2048]{2,1,0:T(8,128)S(1)} %fusion.146, f32[4,512]{1,0:T(4,128)S(1)} %dynamic-slice_bitcast_fusion.2, pred[512,2048]{1,0:T(8,128)(4,1)S(1)} %fusion.147, bf16[2048,4,64]{0,2,1:T(8,128)(2,1)} %get-tuple-element.638, ...), kind=kOutput, calls=%fused_computation.28.clone.1 | convolution fusion | flops 557840384 | bytes 35930116 | tf_op jit(solution)/shard_map/while/body/eval_jaxpr/qhd,khd->hqk/dot_general | solution.py:175
  623.0 10.9 multiply_convert_fusion.8
  634.0 7.2 fusion.148
  641.2 8.5 fusion.149
  669.0 8.2 reshape.383
  677.3 9.5 pad_maximum_fusion.3
  686.7 18.7 %gather_fusion.3 = bf16[2048,3,256]{2,1,0:T(4,128)(2,1)} fusion(bf16[2048,3,256]{2,1,0:T(4,128)(2,1)} %pad_maximum_fusion.3, s32[2048]{0:T(1024)S(1)} %copy-done.25), kind=kCustom, calls=%fused_computation.3 | custom fusion | bytes 6299648 | tf_op jit(solution)/shard_map/gather | solution.py:209
  705.4 51.5 %all_to_all.60 = bf16[2048,3,1,256]{3,1,2,0:T(4,128)(2,1)S(1)} all-to-all(bf16[2048,3,1,256]{3,1,2,0:T(4,128)(2,1)} %bitcast.213), channel_id=1, replica_groups=mesh['seq'=4,'fsdp'=8] {'seq'}, dimensions={0} | all-to-all | bytes 6291456 | tf_op jit(solution)/shard_map/all_to_all | solution.py:210
  760.2 8.5 convolution_convert_fusion.1
  770.4 16.6 %convolution_convert_fusion = bf16[1024,8192]{1,0:T(8,128)(2,1)} fusion(bf16[512,4096]{1,0:T(8,128)(2,1)} %get-tuple-element.412, bf16[512,4096]{1,0:T(8,128)(2,1)} %get-tuple-element.411, f32[512,1024]{1,0:T(8,128)S(1)} %copy-done.12, f32[1024]{0:T(1024)S(1)} %bitcast.237, f32[512]{0:T(512)S(1)} %copy-done.36), kind=kOutput, calls=%fused_computation.63 | convolution fusion | flops 8616673280 | bytes 27269120 | tf_op jit(solution)/shard_map/rd,rf->df/dot_general | solution.py:139
  789.6 45.9 %reduce-scatter.7.cloned.1.call-done = bf16[128,3072]{1,0:T(8,128)(2,1)} async-done(((bf16[1024,3072]{1,0:T(8,128)(2,1)}), bf16[128,3072]{1,0:T(8,128)(2,1)}) %reduce-scatter.7.cloned.1.call-update) | async-done | bytes 786448 | tf_op jit(solution)/shard_map/reduce_scatter | solution.py:223
  835.4 169.0 %reduce-scatter.11.cloned.1.call-done = bf16[128,8192]{1,0:T(8,128)(2,1)} async-done(((bf16[1024,8192]{1,0:T(8,128)(2,1)}), bf16[128,8192]{1,0:T(8,128)(2,1)}) %reduce-scatter.11.cloned.1.call-update) | async-done | bytes 2097168 | tf_op jit(solution)/shard_map/reduce_scatter | solution.py:234
  1005.7 10.3 fusion.69
  1016.0 8.0 fusion.66
  1024.0 13.6 %all-reduce.2 = (bf16[1024]{0:T(1024)(128)(2,1)S(1)}, bf16[1024]{0:T(1024)(128)(2,1)S(1)}) all-reduce(bf16[1024]{0:T(1024)(128)(2,1)S(1)} %get-tuple-element.351, bf16[1024]{0:T(1024)(128)(2,1)S(1)} %copy-done.38), channel_id=2, replica_groups=mesh['seq'=4,'fsdp'=8] {'fsdp'}, use_global_device_ids=true, to_apply=%region_14.15.clone | all-reduce | flops 2048 | bytes 8192
  1037.8 10.2 all-reduce.3
  1052.1 59.8 %all-reduce.7.cloned.1.call-done = (bf16[128,4096]{0,1:T(8,128)(2,1)}, bf16[128,3072]{1,0:T(8,128)(2,1)}, bf16[128,1024]{1,0:T(8,128)(2,1)}, bf16[128,8192]{1,0:T(8,128)(2,1)}) async-done(((bf16[128,4096]{0,1:T(8,128)(2,1)}, bf16[128,3072]{1,0:T(8,128)(2,1)}, bf16[128,1024]{1,0:T(8,128)(2,1)}, bf16[128,8192]{1,0:T(8,128)(2,1)}), (bf16[128,4096]{0,1:T(8,128)(2,1)}, bf16[128,3072]{1,0:T(8,128)(2,1)}, ...) | async-done | bytes 4194320 | tf_op jit(solution)/shard_map/psum | solution.py:247
  (301 shorter events, 260.2 us)
Async XLA Ops:
  7.2 70.6 %all-gather.7.cloned.1.call-start = ((), (), s32[]{:S(2)}) async-start(), calls=%async_computation.8 | async-start | bytes 7077888 | tf_op jit(solution)/shard_map/all_gather | solution.py:52
  9.6 295.9 %all-gather.9.cloned.1.call-start = ((), (), s32[]{:S(2)}) async-start(), calls=%async_computation.9 | async-start | bytes 2359296 | tf_op jit(solution)/shard_map/all_gather | solution.py:53
  11.5 17.4 %copy-start.7 = (bf16[1,512,1024]{2,1,0:T(8,128)(2,1)S(1)}, bf16[1,512,1024]{2,1,0:T(8,128)(2,1)}, u32[]{:S(2)}) copy-start(bf16[1,512,1024]{2,1,0:T(8,128)(2,1)} %param.15) | copy-start | bytes 3145732
  11.5 298.6 %all-gather.11.cloned.1.call-start = ((), (), s32[]{:S(2)}) async-start(), calls=%async_computation.10 | async-start | bytes 18874368 | tf_op jit(solution)/shard_map/all_gather | solution.py:111
  28.9 48.8 %copy-start.30 = (f32[8,1,128]{2,1,0:T(1,128)}, f32[8,1,128]{2,1,0:T(1,128)S(1)}, u32[]{:S(2)}) copy-start(f32[8,1,128]{2,1,0:T(1,128)S(1)} %convert_element_type.214) | copy-start | bytes 12292
  29.8 47.9 %copy-start.33 = (f32[512]{0:T(512)}, f32[512]{0:T(512)S(1)}, u32[]{:S(2)}) copy-start(f32[512]{0:T(512)S(1)} %get-tuple-element.418) | copy-start | bytes 6148
  95.2 7.4 copy-start.37
  95.2 40.6 %all-to-all-start = ((bf16[512,3,4,256]{0,3,1,2:T(8,128)(2,1)}), bf16[512,3,4,256]{0,3,1,2:T(8,128)(2,1)S(1)}, u32[]{:S(2)}, u32[]{:S(2)}) async-start(bf16[512,3,4,256]{0,3,1,2:T(8,128)(2,1)} %copy.114), calls=%async_computation | async-start | bytes 6291456 | tf_op jit(solution)/shard_map/all_to_all | solution.py:58
  99.1 243.2 %all-gather.13.cloned.1.call-start = ((), (), s32[]{:S(2)}) async-start(), calls=%async_computation.11 | async-start | bytes 9437184 | tf_op jit(solution)/shard_map/all_gather | solution.py:112
  112.3 41.2 %copy-start.26 = (s32[2048]{0:T(1024)}, s32[2048]{0:T(1024)S(1)}, u32[]{:S(2)}) copy-start(s32[2048]{0:T(1024)S(1)} %fusion.84) | copy-start | bytes 24580
  256.1 8.6 copy-start.24
  273.7 9.2 copy-start.42
  278.5 17.8 %all-to-all-start.1 = ((bf16[4,2,65536]{2,1,0:T(2,128)(2,1)}), bf16[4,2,65536]{2,1,0:T(2,128)(2,1)}, u32[]{:S(2)}, u32[]{:S(2)}) async-start(bf16[4,2,65536]{2,1,0:T(2,128)(2,1)} %reshape.393), calls=%async_computation.1 | async-start | bytes 2097152 | tf_op jit(solution)/shard_map/all_to_all | solution.py:105
  282.8 504.3 %reduce-scatter.13.cloned.1.call-start = ((), (), s32[]{:S(2)}) async-start(), calls=%async_computation.15 | async-start | bytes 9437184
  292.7 103.2 %copy-start.28 = (f32[8,1,128]{2,1,0:T(1,128)}, f32[8,1,128]{2,1,0:T(1,128)S(1)}, u32[]{:S(2)}) copy-start(f32[8,1,128]{2,1,0:T(1,128)S(1)} %convert_element_type.215) | copy-start | bytes 12292
  292.7 12.8 %copy-start.8 = (bf16[1,512,1024]{2,1,0:T(8,128)(2,1)S(1)}, bf16[1,512,1024]{2,1,0:T(8,128)(2,1)}, u32[]{:S(2)}) copy-start(bf16[1,512,1024]{2,1,0:T(8,128)(2,1)} %param.15) | copy-start | bytes 3145732
  310.0 85.9 %copy-start.35 = (f32[512]{0:T(512)}, f32[512]{0:T(512)S(1)}, u32[]{:S(2)}) copy-start(f32[512]{0:T(512)S(1)} %get-tuple-element.420) | copy-start | bytes 6148
  310.1 32.2 %copy-start.22 = (bf16[1,512,1024]{2,1,0:T(8,128)(2,1)S(1)}, bf16[1,512,1024]{2,1,0:T(8,128)(2,1)}, u32[]{:S(2)}) copy-start(bf16[1,512,1024]{2,1,0:T(8,128)(2,1)} %param.22) | copy-start | bytes 3145732
  402.8 17.9 %all-to-all-start.2 = ((bf16[512,4,256]{0,2,1:T(8,128)(2,1)}), bf16[512,4,256]{0,2,1:T(8,128)(2,1)S(1)}, u32[]{:S(2)}, u32[]{:S(2)}) async-start(bf16[512,4,256]{0,2,1:T(8,128)(2,1)} %bitcast.222), calls=%async_computation.2 | async-start | bytes 2097152 | tf_op jit(solution)/shard_map/all_to_all | solution.py:159
  406.5 383.0 %reduce-scatter.9.cloned.1.call-start = ((), (), s32[]{:S(2)}) async-start(), calls=%async_computation.13 | async-start | bytes 2359296 | tf_op jit(solution)/shard_map/reduce_scatter | solution.py:226
  411.1 13.9 %copy-start.27 = (s32[2048]{0:T(1024)S(1)}, s32[2048]{0:T(1024)}, u32[]{:S(2)}) copy-start(s32[2048]{0:T(1024)} %copy-done.26) | copy-start | bytes 24580
  411.1 424.3 %reduce-scatter.7.cloned.1.call-start = ((), (), s32[]{:S(2)}) async-start(), calls=%async_computation.12 | async-start | bytes 7077888 | tf_op jit(solution)/shard_map/reduce_scatter | solution.py:223
  450.9 15.8 %copy-start = (f32[4,512,2048]{2,1,0:T(8,128)}, f32[4,512,2048]{2,1,0:T(8,128)S(1)}, u32[]{:S(2)}) copy-start(f32[4,512,2048]{2,1,0:T(8,128)S(1)} %fusion.146) | copy-start | bytes 50331652 | tf_op jit(solution)/shard_map/while
  477.7 15.3 %slice-start = ((s8[8388608]{0:T(1024)(128)(4,1)}), s8[4194304]{0:T(1024)(128)(4,1)S(1)}, s32[]{:S(2)}) async-start(s8[8388608]{0:T(1024)(128)(4,1)} %bitcast.211), calls=%async_computation.17 | async-start | bytes 8388608 | tf_op jit(solution)/shard_map/while
  484.4 8.6 slice-start.1
  502.8 15.8 %copy-start = (f32[4,512,2048]{2,1,0:T(8,128)}, f32[4,512,2048]{2,1,0:T(8,128)S(1)}, u32[]{:S(2)}) copy-start(f32[4,512,2048]{2,1,0:T(8,128)S(1)} %fusion.146) | copy-start | bytes 50331652 | tf_op jit(solution)/shard_map/while
  529.5 7.2 copy-start.17
  529.5 15.7 %slice-start = ((s8[8388608]{0:T(1024)(128)(4,1)}), s8[4194304]{0:T(1024)(128)(4,1)S(1)}, s32[]{:S(2)}) async-start(s8[8388608]{0:T(1024)(128)(4,1)} %bitcast.211), calls=%async_computation.17 | async-start | bytes 8388608 | tf_op jit(solution)/shard_map/while
  536.8 8.5 slice-start.1
  555.0 15.8 %copy-start = (f32[4,512,2048]{2,1,0:T(8,128)}, f32[4,512,2048]{2,1,0:T(8,128)S(1)}, u32[]{:S(2)}) copy-start(f32[4,512,2048]{2,1,0:T(8,128)S(1)} %fusion.146) | copy-start | bytes 50331652 | tf_op jit(solution)/shard_map/while
  581.7 7.2 copy-start.17
  581.8 15.7 %slice-start = ((s8[8388608]{0:T(1024)(128)(4,1)}), s8[4194304]{0:T(1024)(128)(4,1)S(1)}, s32[]{:S(2)}) async-start(s8[8388608]{0:T(1024)(128)(4,1)} %bitcast.211), calls=%async_computation.17 | async-start | bytes 8388608 | tf_op jit(solution)/shard_map/while
  589.0 8.5 slice-start.1
  607.2 15.8 %copy-start = (f32[4,512,2048]{2,1,0:T(8,128)}, f32[4,512,2048]{2,1,0:T(8,128)S(1)}, u32[]{:S(2)}) copy-start(f32[4,512,2048]{2,1,0:T(8,128)S(1)} %fusion.146) | copy-start | bytes 50331652 | tf_op jit(solution)/shard_map/while
  634.0 7.2 copy-start.17
  634.0 15.7 %slice-start = ((s8[8388608]{0:T(1024)(128)(4,1)}), s8[4194304]{0:T(1024)(128)(4,1)S(1)}, s32[]{:S(2)}) async-start(s8[8388608]{0:T(1024)(128)(4,1)} %bitcast.211), calls=%async_computation.17 | async-start | bytes 8388608 | tf_op jit(solution)/shard_map/while
  641.2 8.5 slice-start.1
  664.8 12.4 %copy-start.13 = (bf16[2048,1,256]{2,1,0:T(2,128)(2,1)S(1)}, bf16[2048,1,256]{2,1,0:T(2,128)(2,1)}, u32[]{:S(2)}) copy-start(bf16[2048,1,256]{2,1,0:T(2,128)(2,1)} %copy.136) | copy-start | bytes 3145732
  677.3 9.5 copy-start.25
  768.8 235.6 %reduce-scatter.11.cloned.1.call-start = ((), (), s32[]{:S(2)}) async-start(), calls=%async_computation.14 | async-start | bytes 18874368 | tf_op jit(solution)/shard_map/reduce_scatter | solution.py:234
  787.0 217.4 %copy-start.43 = (u32[32]{0:T(128)S(1)}, u32[32]{0:T(128)}, u32[]{:S(2)}) copy-start(u32[32]{0:T(128)} %constant.73) | copy-start | bytes 388
  787.0 324.9 %all-reduce.7.cloned.1.call-start = ((), (), s32[]{:S(2)}) async-start(), calls=%async_computation.16 | async-start | bytes 8388608 | tf_op jit(solution)/shard_map/psum | solution.py:247
  1005.7 10.3 copy-start.9
  1005.7 10.3 copy-start.15
  1016.0 8.0 copy-start.38
  1016.0 33.0 %copy-start.11 = (f32[512,1024]{1,0:T(8,128)S(1)}, f32[512,1024]{1,0:T(8,128)}, u32[]{:S(2)}) copy-start(f32[512,1024]{1,0:T(8,128)} %copy-done.10) | copy-start | bytes 6291460
  1016.0 33.0 %copy-start.32 = (f32[512]{0:T(512)S(1)}, f32[512]{0:T(512)}, u32[]{:S(2)}) copy-start(f32[512]{0:T(512)} %get-tuple-element.417) | copy-start | bytes 6148
  1111.9 6.8 copy-start.23
  (44 other events, 178.8 us)
Sparse Core Ops, SparseCore 0:
  10.2 67.4 all-gather.6
  79.9 27.7 all-gather.8
  109.3 150.5 all-gather.10
  261.9 80.2 all-gather.12
  378.0 88.1 reduce-scatter.12
  468.4 34.2 reduce-scatter.8
  768.9 66.4 reduce-scatter.6
  837.8 166.5 reduce-scatter.10
  1008.7 103.2 all-reduce.6
where the time goes:
time: 1140 us; the launch traced here: 1130 us
  waiting for transfers between devices  373 us (33%)
  matrix products  303 us (27%)
  local copies, waits for them, and re-layouts  207 us (18%)
  other arithmetic  117 us (10%)
  blocking collectives  98.6 us (9%)
  between operations  15.1 us (1%)
  starting transfers between devices  12.2 us (1%)
    reduce_scatter x1, waiting for transfers between devices, on_device(): lax.psum_scatter(grad_gate_up_term.astype(jnp.bfloat16), 'fsdp', scatter_...  169 us
    psum x1, waiting for transfers between devices, on_device(): lax.psum(mlp_shards[2].astype(jnp.bfloat16), 'seq').astype(jnp.float32)  59.8 us
    all_to_all x1, blocking collectives, on_device(): lax.all_to_all(dealt_grad.reshape(group_len, 3, 1, -1), 'seq', split_axis...  51.5 us
    dot_general x4, matrix products, backward_block(): jnp.einsum('qhd,khd->hqk', grad_blk, values, preferred_element_type=jnp.f...  49.3 us
    all_gather x1, waiting for transfers between devices, on_device(): lax.all_gather(weight_qkv.astype(jnp.bfloat16), 'fsdp', axis=0, tiled=True)  47.9 us
    reduce_scatter x1, waiting for transfers between devices, on_device(): lax.psum_scatter(grad_qkv_term.astype(jnp.bfloat16), 'fsdp', scatter_dime...  45.9 us
    unnamed x85, local copies, waits for them, and re-layouts  44.8 us
    convert_element_type x4, other arithmetic, backward_block(): grad_score = (probability * (grad_prob - row_delta)).astype(jnp.bfloat16)  43.7 us
  transfers between devices with their start and end apart: 12, of which 8 were waited for; matrix products, arithmetic and copies ran while one was open for 51% of the time, Pallas kernels for 0%

commit v1 on v0

--- a/solution.py
+++ b/solution.py
@@ -2,6 +2,7 @@
 import jax.numpy as jnp
 from jax import lax
 from jax.sharding import PartitionSpec as P
+from jax.lax import all_gather
 
 HEADS = 16
 HEAD_DIM = 64
@@ -244,7 +245,9 @@
         lax.psum(attn_shards[2].astype(jnp.bfloat16), "seq").astype(jnp.float32),
         lax.psum(mlp_shards[0].astype(jnp.bfloat16), "seq").astype(jnp.float32),
         lax.psum(mlp_shards[1].astype(jnp.bfloat16), "seq").astype(jnp.float32),
-        lax.psum(mlp_shards[2].astype(jnp.bfloat16), "seq").astype(jnp.float32),
+        jnp.sum(all_gather(mlp_shards[2].astype(jnp.bfloat16), axis_name="seq"), axis=0).astype(
+            jnp.float32
+        ),
     )
     return (
         result_rows[None],

time: 1140 us -> 1170 us (1.026)
  other arithmetic: 117 us -> 140 us
    reduce_sum x0 -> x1, other arithmetic: none -> 23 us  [on_device(): jnp.sum(all_gather(mlp_shards[2].astype(jnp.bfloat16), axis_name='seq'),...]
    unnamed x85 -> x83, local copies, waits for them, and re-layouts: 44.8 us -> 44.5 us
  transfers between devices with their start and end apart: 12 -> 13, of which waited for: 8 -> 9; matrix products, arithmetic and copies ran while one was open for 51% -> 52% of each run, Pallas kernels for 0% -> 0%
where the time goes in v1:
time: 1170 us; the launch traced here: 1160 us
  waiting for transfers between devices  378 us (32%)
  matrix products  304 us (26%)
  local copies, waits for them, and re-layouts  213 us (18%)
  other arithmetic  140 us (12%)
  blocking collectives  99.2 us (8%)
  between operations  15.4 us (1%)
  starting transfers between devices  12.2 us (1%)
    reduce_scatter x1, waiting for transfers between devices, on_device(): lax.psum_scatter(grad_gate_up_term.astype(jnp.bfloat16), 'fsdp', scatter_...  169 us
    psum x1, waiting for transfers between devices, on_device(): lax.psum(attn_shards[1].astype(jnp.bfloat16), 'seq').astype(jnp.float32)  59.3 us
    all_to_all x1, blocking collectives, on_device(): lax.all_to_all(dealt_grad.reshape(group_len, 3, 1, -1), 'seq', split_axis...  51.6 us
    dot_general x4, matrix products, backward_block(): jnp.einsum('qhd,khd->hqk', grad_blk, values, preferred_element_type=jnp.f...  49.3 us
    all_gather x1, waiting for transfers between devices, on_device(): lax.all_gather(weight_qkv.astype(jnp.bfloat16), 'fsdp', axis=0, tiled=True)  47.9 us
    unnamed x83, local copies, waits for them, and re-layouts  44.5 us
    reduce_scatter x1, waiting for transfers between devices, on_device(): lax.psum_scatter(grad_qkv_term.astype(jnp.bfloat16), 'fsdp', scatter_dime...  44.4 us
    convert_element_type x4, other arithmetic, backward_block(): grad_score = (probability * (grad_prob - row_delta)).astype(jnp.bfloat16)  43.8 us
  transfers between devices with their start and end apart: 13, of which 9 were waited for; matrix products, arithmetic and copies ran while one was open for 52% of the time, Pallas kernels for 0%

profile of v1, /device:TPU:0, one launch (start us, length us, event | category | flops | bytes accessed | tf_op | source)
XLA Modules:
  0.0 1162.7 jit_solution(18437802570399786372)
XLA Ops:
  15.4 13.5 %all-gather.1 = bf16[8,1,128]{2,1,0:T(2,128)(2,1)S(1)} all-gather(bf16[1,1,128]{2,1,0:T(2,128)(2,1)S(1)} %convert_bitcast_fusion.3), channel_id=1, replica_groups=mesh['seq'=4,'fsdp'=8] {'fsdp'}, dimensions={0}, use_global_device_ids=true | all-gather | bytes 2304 | tf_op jit(solution)/shard_map/all_gather | solution.py:52
  29.8 47.9 %all-gather.9.cloned.1.call-done = bf16[1024,3072]{1,0:T(8,128)(2,1)} async-done(((bf16[128,3072]{1,0:T(8,128)(2,1)}), bf16[1024,3072]{1,0:T(8,128)(2,1)}) %all-gather.9.cloned.1.call-update) | async-done | bytes 6291472 | tf_op jit(solution)/shard_map/all_gather | solution.py:53
  77.7 7.7 convolution_convert_fusion.2
  102.6 8.2 scatter_custom_fusion
  112.0 23.8 %all-to-all-done = bf16[512,3,4,256]{0,3,1,2:T(8,128)(2,1)S(1)} async-done(((bf16[512,3,4,256]{0,3,1,2:T(8,128)(2,1)}), bf16[512,3,4,256]{0,3,1,2:T(8,128)(2,1)S(1)}, u32[]{:S(2)}, u32[]{:S(2)}) %all-to-all-start) | async-done | bytes 3145760 | tf_op jit(solution)/shard_map/all_to_all | solution.py:59
  140.4 13.1 %reshape.381 = bf16[2048,3,4,64]{3,2,1,0:T(4,128)(2,1)} reshape(bf16[4,512,3,1,256]{4,2,1,0,3:T(4,128)(2,1)} %copy.138) | data formatting | bytes 6291456 | tf_op jit(solution)/shard_map/reshape | solution.py:66
  153.6 23.0 %gather_fusion = bf16[2048,3,4,64]{3,2,1,0:T(4,128)(2,1)} fusion(bf16[2048,3,4,64]{3,2,1,0:T(4,128)(2,1)} %reshape.381, s32[2048]{0:T(1024)S(1)} %fusion.84), kind=kCustom, calls=%fused_computation | custom fusion | bytes 6299648 | tf_op jit(solution)/shard_map/gather | solution.py:70
  191.8 64.2 %while.28 = (s32[]{:T(128)}, bf16[4,512,4,64]{1,3,2,0:T(8,128)(2,1)}, f32[4,4,512]{2,1,0:T(4,128)}, s32[4,512]{1,0:T(4,128)}, s32[2048]{0:T(1024)S(1)}, /*index=...) while((s32[]{:T(128)}, ...), condition=%wide.region_6.7_spmd.clone, body=%wide.region_3.6_spmd.clone.sunk | while | flops 1127348224 | bytes 57233532 | solution.py:104
  264.6 9.1 gather_fusion.1
  282.9 9.7 all-gather.2
  310.2 18.8 %fusion.89 = f32[512,8192]{1,0:T(8,128)} fusion(bf16[1024,8192]{1,0:T(8,128)(2,1)} %all-gather.13.cloned.1.call-done, f32[512,1024]{1,0:T(8,128)} %get-tuple-element.397, f32[1024]{0:T(1024)S(1)} %bitcast.236, f32[512]{0:T(512)S(1)} %get-tuple-element.395), kind=kOutput, calls=%fused_computation.139 | convolution fusion | flops 8591507456 | bytes 35657728 | tf_op jit(solution)/shard_map/dot_general | solution.py:117
  329.0 13.3 %all-gather.15.cloned.1.call-done = bf16[1024,4096]{1,0:T(8,128)(2,1)} async-done(((bf16[128,4096]{1,0:T(8,128)(2,1)}), bf16[1024,4096]{1,0:T(8,128)(2,1)}) %all-gather.15.cloned.1.call-update) | async-done | bytes 8388624 | tf_op jit(solution)/shard_map/all_gather | solution.py:113
  342.3 15.1 %multiply_convert_fusion.2 = (bf16[512,4096]{1,0:T(8,128)(2,1)}, bf16[512,4096]{1,0:T(8,128)(2,1)}, bf16[512,4096]{1,0:T(8,128)(2,1)S(1)}) fusion(f32[512,8192]{1,0:T(8,128)} %fusion.89, bf16[1024,4096]{1,0:T(8,128)(2,1)} %all-gather.15.cloned.1.call-done, bf16[1,512,1024]{2,1,0:T(8,128)(2,1)S(1)} %copy-done.22), kind=kOutput, calls=%fused_computation.67 | convolution fusion | flops 4326424576 | bytes 38797312 | tf_op jit(solution)/shard_map/dot_general | solution.py:136
  366.2 11.5 copy.148
  377.8 18.2 %multiply_reduce_fusion.1 = (bf16[1024]{0:T(1024)(128)(2,1)}, f32[512]{0:T(512)S(1)}, f32[512,1024]{1,0:T(8,128)}) fusion(f32[512,1024]{1,0:T(8,128)} %get-tuple-element.397, f32[512]{0:T(512)S(1)} %get-tuple-element.395, f32[1024]{0:T(1024)S(1)} %bitcast.237, bf16[1024,8192]{1,0:T(8,128)(2,1)} %all-gather.13.cloned.1.call-done, ...), kind=kOutput, calls=%fused_computation.97 | convolution fusion | flops 8609855488 | bytes 29370368 | tf_op jit(solution)/shard_map/rf,df->rd/dot_general | solution.py:143
  411.2 9.6 all-to-all-done.2
  425.1 16.1 %gather_fusion.2 = bf16[2048,4,64]{2,1,0:T(4,128)(2,1)} fusion(bf16[2048,4,64]{2,1,0:T(4,128)(2,1)} %reshape.383, s32[2048]{0:T(1024)S(1)} %copy-done.26), kind=kCustom, calls=%fused_computation.2 | custom fusion | bytes 2105344 | tf_op jit(solution)/shard_map/gather | solution.py:163
  446.3 208.9 %while.29 = (s32[]{:T(128)}, f32[2048,4,64]{0,2,1:T(8,128)}, f32[2048,4,64]{0,2,1:T(8,128)}, bf16[4,512,4,64]{1,3,2,0:T(8,128)(2,1)}, bf16[4,512,4,64]{1,3,2,0:T...) while((s32[]{:T(128)}, f32[2048,4,64]{0,2,1:T(8,128)}, ...), condition=%wide.region_11.12_spmd.clone, body=%wide.region_9.11_spmd.clone.sunk | while | flops 2753296384 | bytes 268841472 | solution.py:197
  454.2 12.3 %multiply_reduce_fusion.5 = (f32[4,512]{1,0:T(4,128)}, f32[4,512,2048]{2,1,0:T(8,128)}) fusion(f32[4,512,2048]{2,1,0:T(8,128)S(1)} %fusion.146, f32[4,512]{1,0:T(4,128)S(1)} %dynamic-slice_bitcast_fusion.2, pred[512,2048]{1,0:T(8,128)(4,1)S(1)} %fusion.147, bf16[2048,4,64]{0,2,1:T(8,128)(2,1)} %get-tuple-element.613, ...), kind=kOutput, calls=%fused_computation.28.clone.1 | convolution fusion | flops 557840384 | bytes 35930116 | tf_op jit(solution)/shard_map/while/body/eval_jaxpr/qhd,khd->hqk/dot_general | solution.py:176
  466.6 11.0 multiply_convert_fusion.8
  484.2 8.6 fusion.149
  506.1 12.3 %multiply_reduce_fusion.5 = (f32[4,512]{1,0:T(4,128)}, f32[4,512,2048]{2,1,0:T(8,128)}) fusion(f32[4,512,2048]{2,1,0:T(8,128)S(1)} %fusion.146, f32[4,512]{1,0:T(4,128)S(1)} %dynamic-slice_bitcast_fusion.2, pred[512,2048]{1,0:T(8,128)(4,1)S(1)} %fusion.147, bf16[2048,4,64]{0,2,1:T(8,128)(2,1)} %get-tuple-element.613, ...), kind=kOutput, calls=%fused_computation.28.clone.1 | convolution fusion | flops 557840384 | bytes 35930116 | tf_op jit(solution)/shard_map/while/body/eval_jaxpr/qhd,khd->hqk/dot_general | solution.py:176
  518.5 10.9 multiply_convert_fusion.8
  529.4 7.2 fusion.148
  536.6 8.5 fusion.149
  558.3 12.3 %multiply_reduce_fusion.5 = (f32[4,512]{1,0:T(4,128)}, f32[4,512,2048]{2,1,0:T(8,128)}) fusion(f32[4,512,2048]{2,1,0:T(8,128)S(1)} %fusion.146, f32[4,512]{1,0:T(4,128)S(1)} %dynamic-slice_bitcast_fusion.2, pred[512,2048]{1,0:T(8,128)(4,1)S(1)} %fusion.147, bf16[2048,4,64]{0,2,1:T(8,128)(2,1)} %get-tuple-element.613, ...), kind=kOutput, calls=%fused_computation.28.clone.1 | convolution fusion | flops 557840384 | bytes 35930116 | tf_op jit(solution)/shard_map/while/body/eval_jaxpr/qhd,khd->hqk/dot_general | solution.py:176
  570.7 10.9 multiply_convert_fusion.8
  581.6 7.2 fusion.148
  588.8 8.5 fusion.149
  610.5 12.3 %multiply_reduce_fusion.5 = (f32[4,512]{1,0:T(4,128)}, f32[4,512,2048]{2,1,0:T(8,128)}) fusion(f32[4,512,2048]{2,1,0:T(8,128)S(1)} %fusion.146, f32[4,512]{1,0:T(4,128)S(1)} %dynamic-slice_bitcast_fusion.2, pred[512,2048]{1,0:T(8,128)(4,1)S(1)} %fusion.147, bf16[2048,4,64]{0,2,1:T(8,128)(2,1)} %get-tuple-element.613, ...), kind=kOutput, calls=%fused_computation.28.clone.1 | convolution fusion | flops 557840384 | bytes 35930116 | tf_op jit(solution)/shard_map/while/body/eval_jaxpr/qhd,khd->hqk/dot_general | solution.py:176
  622.9 10.9 multiply_convert_fusion.8
  633.8 7.2 fusion.148
  641.0 8.5 fusion.149
  668.9 8.2 reshape.384
  677.1 9.5 pad_maximum_fusion.3
  686.6 18.7 %gather_fusion.3 = bf16[2048,3,256]{2,1,0:T(4,128)(2,1)} fusion(bf16[2048,3,256]{2,1,0:T(4,128)(2,1)} %pad_maximum_fusion.3, s32[2048]{0:T(1024)S(1)} %copy-done.24), kind=kCustom, calls=%fused_computation.3 | custom fusion | bytes 6299648 | tf_op jit(solution)/shard_map/gather | solution.py:210
  705.4 51.6 %all_to_all.60 = bf16[2048,3,1,256]{3,1,2,0:T(4,128)(2,1)S(1)} all-to-all(bf16[2048,3,1,256]{3,1,2,0:T(4,128)(2,1)} %bitcast.215), channel_id=1, replica_groups=mesh['seq'=4,'fsdp'=8] {'seq'}, dimensions={0} | all-to-all | bytes 6291456 | tf_op jit(solution)/shard_map/all_to_all | solution.py:211
  760.2 8.5 convolution_convert_fusion.1
  770.4 16.9 %convolution_convert_fusion = bf16[1024,8192]{1,0:T(8,128)(2,1)} fusion(bf16[512,4096]{1,0:T(8,128)(2,1)} %get-tuple-element.387, bf16[512,4096]{1,0:T(8,128)(2,1)} %get-tuple-element.386, f32[512,1024]{1,0:T(8,128)S(1)} %copy-done.12, f32[1024]{0:T(1024)S(1)} %bitcast.239, f32[512]{0:T(512)S(1)} %copy-done.35), kind=kOutput, calls=%fused_computation.63 | convolution fusion | flops 8616673280 | bytes 27269120 | tf_op jit(solution)/shard_map/rd,rf->df/dot_general | solution.py:140
  791.0 44.4 %reduce-scatter.7.cloned.1.call-done = bf16[128,3072]{1,0:T(8,128)(2,1)} async-done(((bf16[1024,3072]{1,0:T(8,128)(2,1)}), bf16[128,3072]{1,0:T(8,128)(2,1)}) %reduce-scatter.7.cloned.1.call-update) | async-done | bytes 786448 | tf_op jit(solution)/shard_map/reduce_scatter | solution.py:224
  835.4 169.0 %reduce-scatter.11.cloned.1.call-done = bf16[128,8192]{1,0:T(8,128)(2,1)} async-done(((bf16[1024,8192]{1,0:T(8,128)(2,1)}), bf16[128,8192]{1,0:T(8,128)(2,1)}) %reduce-scatter.11.cloned.1.call-update) | async-done | bytes 2097168 | tf_op jit(solution)/shard_map/reduce_scatter | solution.py:235
  1004.5 10.3 fusion.69
  1014.8 8.1 fusion.66
  1022.9 13.9 %all-reduce.2 = (bf16[1024]{0:T(1024)(128)(2,1)S(1)}, bf16[1024]{0:T(1024)(128)(2,1)S(1)}) all-reduce(bf16[1024]{0:T(1024)(128)(2,1)S(1)} %get-tuple-element.327, bf16[1024]{0:T(1024)(128)(2,1)S(1)} %copy-done.37), channel_id=3, replica_groups=mesh['seq'=4,'fsdp'=8] {'fsdp'}, use_global_device_ids=true, to_apply=%region_14.15.clone | all-reduce | flops 2048 | bytes 8192
  1037.0 10.5 all-reduce.3
  1058.0 6.9 reshape.372
  1064.9 23.0 %reduce_sum.100 = bf16[128,4096]{0,1:T(8,128)(2,1)S(1)} reduce(bf16[4,128,4096]{1,0,2:T(4,128)(2,1)} %reshape.372, bf16[]{:T(256)} %constant.60.clone.1), dimensions={0}, to_apply=%region_26.27 | reduce | flops 1572864 | bytes 5242882 | tf_op jit(solution)/shard_map/reduce_sum | solution.py:248
  1089.5 59.3 %all-reduce.7.cloned.1.call-done = (bf16[128,3072]{1,0:T(8,128)(2,1)}, bf16[128,1024]{1,0:T(8,128)(2,1)}, bf16[128,8192]{1,0:T(8,128)(2,1)}) async-done(((bf16[128,3072]{1,0:T(8,128)(2,1)}, bf16[128,1024]{1,0:T(8,128)(2,1)}, bf16[128,8192]{1,0:T(8,128)(2,1)}), (bf16[128,3072]{1,0:T(8,128)(2,1)}, bf16[128,1024]{1,0:T(8,128)(2,1)}, bf16[128,8192]{1,0:T(8,128)(2,1)})) %all-reduce.7.cloned.1.call-update) | async-done | bytes 3145744 | tf_op jit(solution)/shard_map/psum | solution.py:244
  (304 shorter events, 280.1 us)
Async XLA Ops:
  7.2 70.6 %all-gather.9.cloned.1.call-start = ((), (), s32[]{:S(2)}) async-start(), calls=%async_computation.8 | async-start | bytes 7077888 | tf_op jit(solution)/shard_map/all_gather | solution.py:53
  9.6 296.0 %all-gather.11.cloned.1.call-start = ((), (), s32[]{:S(2)}) async-start(), calls=%async_computation.9 | async-start | bytes 2359296 | tf_op jit(solution)/shard_map/all_gather | solution.py:54
  11.5 17.4 %copy-start.7 = (bf16[1,512,1024]{2,1,0:T(8,128)(2,1)S(1)}, bf16[1,512,1024]{2,1,0:T(8,128)(2,1)}, u32[]{:S(2)}) copy-start(bf16[1,512,1024]{2,1,0:T(8,128)(2,1)} %param.15) | copy-start | bytes 3145732
  11.5 298.6 %all-gather.13.cloned.1.call-start = ((), (), s32[]{:S(2)}) async-start(), calls=%async_computation.10 | async-start | bytes 18874368 | tf_op jit(solution)/shard_map/all_gather | solution.py:112
  28.9 48.8 %copy-start.29 = (f32[8,1,128]{2,1,0:T(1,128)}, f32[8,1,128]{2,1,0:T(1,128)S(1)}, u32[]{:S(2)}) copy-start(f32[8,1,128]{2,1,0:T(1,128)S(1)} %convert_element_type.216) | copy-start | bytes 12292
  29.8 47.9 %copy-start.32 = (f32[512]{0:T(512)}, f32[512]{0:T(512)S(1)}, u32[]{:S(2)}) copy-start(f32[512]{0:T(512)S(1)} %get-tuple-element.393) | copy-start | bytes 6148
  95.2 7.4 copy-start.36
  95.2 40.6 %all-to-all-start = ((bf16[512,3,4,256]{0,3,1,2:T(8,128)(2,1)}), bf16[512,3,4,256]{0,3,1,2:T(8,128)(2,1)S(1)}, u32[]{:S(2)}, u32[]{:S(2)}) async-start(bf16[512,3,4,256]{0,3,1,2:T(8,128)(2,1)} %copy.111), calls=%async_computation | async-start | bytes 6291456 | tf_op jit(solution)/shard_map/all_to_all | solution.py:59
  99.1 243.2 %all-gather.15.cloned.1.call-start = ((), (), s32[]{:S(2)}) async-start(), calls=%async_computation.11 | async-start | bytes 9437184 | tf_op jit(solution)/shard_map/all_gather | solution.py:113
  112.0 41.5 %copy-start.25 = (s32[2048]{0:T(1024)}, s32[2048]{0:T(1024)S(1)}, u32[]{:S(2)}) copy-start(s32[2048]{0:T(1024)S(1)} %fusion.84) | copy-start | bytes 24580
  256.1 8.6 copy-start.23
  273.7 9.2 copy-start.41
  278.6 17.8 %all-to-all-start.1 = ((bf16[4,2,65536]{2,1,0:T(2,128)(2,1)}), bf16[4,2,65536]{2,1,0:T(2,128)(2,1)}, u32[]{:S(2)}, u32[]{:S(2)}) async-start(bf16[4,2,65536]{2,1,0:T(2,128)(2,1)} %reshape.394), calls=%async_computation.1 | async-start | bytes 2097152 | tf_op jit(solution)/shard_map/all_to_all | solution.py:106
  282.9 504.5 %reduce-scatter.13.cloned.1.call-start = ((), (), s32[]{:S(2)}) async-start(), calls=%async_computation.16 | async-start | bytes 9437184
  292.7 103.3 %copy-start.27 = (f32[8,1,128]{2,1,0:T(1,128)}, f32[8,1,128]{2,1,0:T(1,128)S(1)}, u32[]{:S(2)}) copy-start(f32[8,1,128]{2,1,0:T(1,128)S(1)} %convert_element_type.217) | copy-start | bytes 12292
  292.7 12.9 %copy-start.8 = (bf16[1,512,1024]{2,1,0:T(8,128)(2,1)S(1)}, bf16[1,512,1024]{2,1,0:T(8,128)(2,1)}, u32[]{:S(2)}) copy-start(bf16[1,512,1024]{2,1,0:T(8,128)(2,1)} %param.15) | copy-start | bytes 3145732
  310.1 85.8 %copy-start.34 = (f32[512]{0:T(512)}, f32[512]{0:T(512)S(1)}, u32[]{:S(2)}) copy-start(f32[512]{0:T(512)S(1)} %get-tuple-element.395) | copy-start | bytes 6148
  310.2 32.1 %copy-start.22 = (bf16[1,512,1024]{2,1,0:T(8,128)(2,1)S(1)}, bf16[1,512,1024]{2,1,0:T(8,128)(2,1)}, u32[]{:S(2)}) copy-start(bf16[1,512,1024]{2,1,0:T(8,128)(2,1)} %param.22) | copy-start | bytes 3145732
  402.9 17.9 %all-to-all-start.2 = ((bf16[512,4,256]{0,2,1:T(8,128)(2,1)}), bf16[512,4,256]{0,2,1:T(8,128)(2,1)S(1)}, u32[]{:S(2)}, u32[]{:S(2)}) async-start(bf16[512,4,256]{0,2,1:T(8,128)(2,1)} %bitcast.224), calls=%async_computation.2 | async-start | bytes 2097152 | tf_op jit(solution)/shard_map/all_to_all | solution.py:160
  406.6 384.4 %reduce-scatter.9.cloned.1.call-start = ((), (), s32[]{:S(2)}) async-start(), calls=%async_computation.13 | async-start | bytes 2359296 | tf_op jit(solution)/shard_map/reduce_scatter | solution.py:227
  411.1 13.9 %copy-start.26 = (s32[2048]{0:T(1024)S(1)}, s32[2048]{0:T(1024)}, u32[]{:S(2)}) copy-start(s32[2048]{0:T(1024)} %copy-done.25) | copy-start | bytes 24580
  411.1 424.3 %reduce-scatter.7.cloned.1.call-start = ((), (), s32[]{:S(2)}) async-start(), calls=%async_computation.12 | async-start | bytes 7077888 | tf_op jit(solution)/shard_map/reduce_scatter | solution.py:224
  450.8 15.8 %copy-start = (f32[4,512,2048]{2,1,0:T(8,128)}, f32[4,512,2048]{2,1,0:T(8,128)S(1)}, u32[]{:S(2)}) copy-start(f32[4,512,2048]{2,1,0:T(8,128)S(1)} %fusion.146) | copy-start | bytes 50331652 | tf_op jit(solution)/shard_map/while
  477.5 6.7 copy-start.17
  477.5 15.3 %slice-start = ((s8[8388608]{0:T(1024)(128)(4,1)}), s8[4194304]{0:T(1024)(128)(4,1)S(1)}, s32[]{:S(2)}) async-start(s8[8388608]{0:T(1024)(128)(4,1)} %bitcast.213), calls=%async_computation.18 | async-start | bytes 8388608 | tf_op jit(solution)/shard_map/while
  484.2 8.6 slice-start.1
  502.6 15.8 %copy-start = (f32[4,512,2048]{2,1,0:T(8,128)}, f32[4,512,2048]{2,1,0:T(8,128)S(1)}, u32[]{:S(2)}) copy-start(f32[4,512,2048]{2,1,0:T(8,128)S(1)} %fusion.146) | copy-start | bytes 50331652 | tf_op jit(solution)/shard_map/while
  529.4 7.2 copy-start.17
  529.4 15.7 %slice-start = ((s8[8388608]{0:T(1024)(128)(4,1)}), s8[4194304]{0:T(1024)(128)(4,1)S(1)}, s32[]{:S(2)}) async-start(s8[8388608]{0:T(1024)(128)(4,1)} %bitcast.213), calls=%async_computation.18 | async-start | bytes 8388608 | tf_op jit(solution)/shard_map/while
  536.6 8.5 slice-start.1
  554.9 15.8 %copy-start = (f32[4,512,2048]{2,1,0:T(8,128)}, f32[4,512,2048]{2,1,0:T(8,128)S(1)}, u32[]{:S(2)}) copy-start(f32[4,512,2048]{2,1,0:T(8,128)S(1)} %fusion.146) | copy-start | bytes 50331652 | tf_op jit(solution)/shard_map/while
  581.6 7.2 copy-start.17
  581.6 15.7 %slice-start = ((s8[8388608]{0:T(1024)(128)(4,1)}), s8[4194304]{0:T(1024)(128)(4,1)S(1)}, s32[]{:S(2)}) async-start(s8[8388608]{0:T(1024)(128)(4,1)} %bitcast.213), calls=%async_computation.18 | async-start | bytes 8388608 | tf_op jit(solution)/shard_map/while
  588.8 8.5 slice-start.1
  607.1 15.8 %copy-start = (f32[4,512,2048]{2,1,0:T(8,128)}, f32[4,512,2048]{2,1,0:T(8,128)S(1)}, u32[]{:S(2)}) copy-start(f32[4,512,2048]{2,1,0:T(8,128)S(1)} %fusion.146) | copy-start | bytes 50331652 | tf_op jit(solution)/shard_map/while
  633.8 7.2 copy-start.17
  633.8 15.7 %slice-start = ((s8[8388608]{0:T(1024)(128)(4,1)}), s8[4194304]{0:T(1024)(128)(4,1)S(1)}, s32[]{:S(2)}) async-start(s8[8388608]{0:T(1024)(128)(4,1)} %bitcast.213), calls=%async_computation.18 | async-start | bytes 8388608 | tf_op jit(solution)/shard_map/while
  641.0 8.5 slice-start.1
  664.7 12.4 %copy-start.13 = (bf16[2048,1,256]{2,1,0:T(2,128)(2,1)S(1)}, bf16[2048,1,256]{2,1,0:T(2,128)(2,1)}, u32[]{:S(2)}) copy-start(bf16[2048,1,256]{2,1,0:T(2,128)(2,1)} %copy.133) | copy-start | bytes 3145732
  677.1 9.5 copy-start.24
  768.8 235.6 %reduce-scatter.11.cloned.1.call-start = ((), (), s32[]{:S(2)}) async-start(), calls=%async_computation.14 | async-start | bytes 18874368 | tf_op jit(solution)/shard_map/reduce_scatter | solution.py:235
  787.3 270.7 %all-gather.17.cloned.1.call-start = ((), (), s32[]{:S(2)}) async-start(), calls=%async_computation.15 | async-start | bytes 5242880 | tf_op jit(solution)/shard_map/all_gather | solution.py:248
  789.7 359.1 %all-reduce.7.cloned.1.call-start = ((), (), s32[]{:S(2)}) async-start(), calls=%async_computation.17 | async-start | bytes 6291456 | tf_op jit(solution)/shard_map/psum | solution.py:244
  1004.4 10.3 copy-start.9
  1004.5 10.3 copy-start.15
  1014.8 8.1 copy-start.37
  1014.8 33.7 %copy-start.11 = (f32[512,1024]{1,0:T(8,128)S(1)}, f32[512,1024]{1,0:T(8,128)}, u32[]{:S(2)}) copy-start(f32[512,1024]{1,0:T(8,128)} %copy-done.10) | copy-start | bytes 6291460
  1014.8 33.7 %copy-start.31 = (f32[512]{0:T(512)S(1)}, f32[512]{0:T(512)}, u32[]{:S(2)}) copy-start(f32[512]{0:T(512)} %get-tuple-element.392) | copy-start | bytes 6148
  (44 other events, 174.5 us)
Sparse Core Ops, SparseCore 0:
  10.2 67.4 all-gather.8
  79.9 27.7 all-gather.10
  109.3 150.5 all-gather.12
  261.9 80.2 all-gather.14
  377.9 88.1 reduce-scatter.12
  468.2 34.1 reduce-scatter.8
  768.9 66.4 reduce-scatter.6
  837.8 166.5 reduce-scatter.10
  1006.8 51.1 all-gather.16
  1061.2 87.5 all-reduce.6
